TPU v7x, 256 devices: a whole 4x4x8 slice. The times are simulated.
256 devices in a mesh: rows: 64 (over z, x, core), coil: 4 (over y).
Axes of the slice: x: 4, y: 4, z: 8, core: 2. Of those that a mesh axis runs over, the one named last changes fastest.
Arguments:
- kspace: float32 [128, 32768], P('coil', 'rows'), may hold values from -6 to 6
- sample_mask: int32 [128, 32768], P('coil', 'rows'), may hold values 0 or 1
- start_basis: float32 [4, 2048, 128], P('coil', 'rows'), may hold values from -6 to 6
Outputs:
- recovered: float32 [128, 32768], P('coil', 'rows')
- basis: float32 [4, 2048, 128], P('coil', 'rows')
All inputs are finite; a program needn't handle non-finite values. No bound on the sum of `sample_mask` on one device may be relied on, other than what follows from the above.
Results may differ from a plain program's by a relative error of at most 0.00011.
Values sent between devices are 32-bit elements; how exact they have to be, the bound alone decides.
A program may use at most 64 MiB of HBM per device.

v0:
```python
import jax
import jax.numpy as jnp
from jax import lax
from jax.sharding import PartitionSpec as P

KER = 64
ITERS = 2
threshold = 0.05


def shifted(block, axis, distance):
    devices = range(lax.axis_size(axis))
    route = [((i - distance) % len(devices), i) for i in devices]
    return lax.ppermute(block, axis, route)


def orthonormal(normal_rows, gram_matrix):
    factor = jnp.linalg.cholesky(gram_matrix)
    return lax.linalg.triangular_solve(
        factor, normal_rows, left_side=False, lower=True, transpose_a=True
    )


def coil_total(partial_value):
    return lax.psum(partial_value, "coil")


def shards(kspace, sample_mask, start_basis):
    highest = lax.Precision.HIGHEST
    channels = kspace.shape[0]
    tile_rows = kspace.shape[1]
    mask_float = sample_mask.astype(jnp.float32)
    sampled = kspace * mask_float
    next_rim = shifted(sampled[:, : KER - 1], "rows", -1)
    extended = jnp.concatenate([sampled, next_rim], axis=1)
    hankel_cols = jnp.stack(
        [extended[:, offset : offset + tile_rows] for offset in range(KER)], axis=0
    )
    hankel_cols = hankel_cols.reshape(KER * channels, tile_rows)
    owned_basis = start_basis.reshape(start_basis.shape[1], start_basis.shape[2])

    def fold_basis(shard_piece):
        return lax.dot_general(
            shard_piece,
            hankel_cols,
            (((0,), (0,)), ((), ())),
            precision=highest,
            preferred_element_type=jnp.float32,
        )

    def apply_hankel(current):
        partial_value = fold_basis(lax.all_gather(current, "rows", axis=0, tiled=True))
        return coil_total(partial_value)

    for iteration in range(ITERS):
        images = apply_hankel(owned_basis)
        normal_rows = lax.psum_scatter(
            lax.dot_general(
                hankel_cols,
                images,
                (((1,), (1,)), ((), ())),
                precision=highest,
                preferred_element_type=jnp.float32,
            ),
            "rows",
            scatter_dimension=0,
            tiled=True,
        )
        local_gram = jnp.dot(
            normal_rows.T, normal_rows, precision=highest, preferred_element_type=jnp.float32
        )
        gram_matrix = lax.psum(local_gram, ("rows", "coil"))
        owned_basis = orthonormal(normal_rows, gram_matrix)
    images = apply_hankel(owned_basis)
    projected = jnp.dot(
        lax.all_gather(owned_basis, "rows", axis=0, tiled=True),
        images,
        precision=highest,
        preferred_element_type=jnp.float32,
    )
    stacked = projected.reshape(KER, channels, tile_rows)
    spread = jnp.zeros((channels, tile_rows + KER - 1), jnp.float32)
    for offset in range(KER):
        spread = spread.at[:, offset : offset + tile_rows].add(stacked[offset])
    carried = shifted(spread[:, tile_rows:], "rows", 1)
    estimate = spread[:, :tile_rows].at[:, : KER - 1].add(carried) / KER
    residual = mask_float * (kspace - estimate)
    recovered = estimate + residual - jnp.clip(residual, -threshold, threshold)
    return (recovered, owned_basis.reshape(1, owned_basis.shape[0], owned_basis.shape[1]))


def solution(mesh):
    return jax.shard_map(
        shards,
        mesh=mesh,
        in_specs=(P("coil", "rows"), P("coil", "rows"), P("coil", "rows", None)),
        out_specs=(P("coil", "rows"), P("coil", "rows", None)),
        check_vma=False,
    )
```

profile of v0, /device:TPU:16, one launch (start us, length us, event | category | flops | bytes accessed | tf_op | source)
XLA Modules:
  0.0 1392.1 jit_solution(3663720347566413571)
XLA Ops:
  8.7 7.5 collective-permute-start
  62.2 28.1 %all-gather.9.cloned.1.call-done = f32[1,2048,128]{2,1,0:T(8,128)} async-done(((f32[1,32,128]{2,1,0:T(8,128)}), f32[1,2048,128]{2,1,0:T(8,128)}) %all-gather.9.cloned.1.call-update) | async-done | bytes 1048592 | tf_op jit(solution)/shard_map/all_gather | solution.py:52
  90.4 9.9 convolution_bitcast_fusion
  100.5 43.9 %all-reduce.7.cloned.1.call-done = f32[128,512]{0,1:T(8,128)} async-done(((f32[128,512]{0,1:T(8,128)}), f32[128,512]{0,1:T(8,128)}) %all-reduce.7.cloned.1.call-update) | async-done | bytes 262160 | tf_op jit(solution)/shard_map/psum | solution.py:25
  144.4 6.6 fusion.135
  151.0 141.7 %reduce-scatter.3.cloned.1.call-done = f32[32,128]{1,0:T(8,128)} async-done(((f32[2048,128]{1,0:T(8,128)}), f32[32,128]{1,0:T(8,128)}) %reduce-scatter.3.cloned.1.call-update) | async-done | bytes 16400 | tf_op jit(solution)/shard_map/reduce_scatter | solution.py:57
  292.7 1.7 fusion.136
  294.5 243.0 %all-reduce.9.cloned.1.call-done = f32[128,128]{0,1:T(8,128)} async-done(((f32[128,128]{0,1:T(8,128)}), f32[128,128]{0,1:T(8,128)}) %all-reduce.9.cloned.1.call-update) | async-done | bytes 65552 | tf_op jit(solution)/shard_map/psum | solution.py:72
  539.3 11.7 cholesky.44
  552.3 9.8 custom-call.6
  563.9 74.0 %all-gather.5.cloned.1.call-done = f32[2048,128]{1,0:T(8,128)} async-done(((f32[32,128]{1,0:T(8,128)}), f32[2048,128]{1,0:T(8,128)}) %all-gather.5.cloned.1.call-update) | async-done | bytes 1048592 | tf_op jit(solution)/shard_map/all_gather | solution.py:52
  637.9 5.8 fusion.137
  643.8 44.0 %all-reduce.11.cloned.1.call-done = f32[128,512]{1,0:T(8,128)} async-done(((f32[128,512]{1,0:T(8,128)}), f32[128,512]{1,0:T(8,128)}) %all-reduce.11.cloned.1.call-update) | async-done | bytes 262160 | tf_op jit(solution)/shard_map/psum | solution.py:25
  687.9 6.6 fusion.138
  694.6 141.7 %reduce-scatter.5.cloned.1.call-done = f32[32,128]{1,0:T(8,128)} async-done(((f32[2048,128]{1,0:T(8,128)}), f32[32,128]{1,0:T(8,128)}) %reduce-scatter.5.cloned.1.call-update) | async-done | bytes 16400 | tf_op jit(solution)/shard_map/reduce_scatter | solution.py:57
  836.3 1.7 fusion.139
  838.5 242.7 %all-reduce.13.cloned.1.call-done = f32[128,128]{0,1:T(8,128)} async-done(((f32[128,128]{0,1:T(8,128)}), f32[128,128]{0,1:T(8,128)}) %all-reduce.13.cloned.1.call-update) | async-done | bytes 65552 | tf_op jit(solution)/shard_map/psum | solution.py:72
  1083.0 11.7 cholesky.55
  1096.0 9.8 custom-call.7
  1107.4 74.2 %all-gather.7.cloned.1.call-done = f32[2048,128]{1,0:T(8,128)} async-done(((f32[32,128]{1,0:T(8,128)}), f32[2048,128]{1,0:T(8,128)}) %all-gather.7.cloned.1.call-update) | async-done | bytes 1048592 | tf_op jit(solution)/shard_map/all_gather | solution.py:76
  1181.6 5.9 fusion.140
  1231.7 4.5 fusion.141
  1321.9 1.6 add_select_fusion.23
  1378.1 5.2 collective-permute-done.1
  (304 shorter events, 243.0 us)
Async XLA Ops:
  7.2 83.2 %all-gather.9.cloned.1.call-start = ((), (), s32[]{:S(2)}) async-start(), calls=%async_computation.11 | async-start | bytes 1064960 | tf_op jit(solution)/shard_map/all_gather | solution.py:52
  8.7 8.9 collective-permute-start
  16.2 128.1 %all-reduce.7.cloned.1.call-start = ((), (), s32[]{:S(2)}) async-start(), calls=%async_computation.2 | async-start | bytes 524288 | tf_op jit(solution)/shard_map/psum | solution.py:25
  100.3 192.4 %reduce-scatter.3.cloned.1.call-start = ((), (), s32[]{:S(2)}) async-start(), calls=%async_computation.3 | async-start | bytes 1064960 | tf_op jit(solution)/shard_map/reduce_scatter | solution.py:57
  151.0 386.5 %all-reduce.9.cloned.1.call-start = ((), (), s32[]{:S(2)}) async-start(), calls=%async_computation.4 | async-start | bytes 131072 | tf_op jit(solution)/shard_map/psum | solution.py:72
  294.4 343.5 %all-gather.5.cloned.1.call-start = ((), (), s32[]{:S(2)}) async-start(), calls=%async_computation.5 | async-start | bytes 1064960 | tf_op jit(solution)/shard_map/all_gather | solution.py:52
  563.7 124.2 %all-reduce.11.cloned.1.call-start = ((), (), s32[]{:S(2)}) async-start(), calls=%async_computation.6 | async-start | bytes 524288 | tf_op jit(solution)/shard_map/psum | solution.py:25
  643.8 192.5 %reduce-scatter.5.cloned.1.call-start = ((), (), s32[]{:S(2)}) async-start(), calls=%async_computation.7 | async-start | bytes 1064960 | tf_op jit(solution)/shard_map/reduce_scatter | solution.py:57
  694.5 386.7 %all-reduce.13.cloned.1.call-start = ((), (), s32[]{:S(2)}) async-start(), calls=%async_computation.8 | async-start | bytes 131072 | tf_op jit(solution)/shard_map/psum | solution.py:72
  838.0 343.6 %all-gather.7.cloned.1.call-start = ((), (), s32[]{:S(2)}) async-start(), calls=%async_computation.9 | async-start | bytes 1064960 | tf_op jit(solution)/shard_map/all_gather | solution.py:76
  1107.4 124.3 %all-reduce.15.cloned.1.call-start = ((), (), s32[]{:S(2)}) async-start(), calls=%async_computation.10 | async-start | bytes 524288 | tf_op jit(solution)/shard_map/psum | solution.py:25
  1181.6 50.0 %copy-start.1 = (f32[2048,128]{1,0:T(8,128)S(1)}, f32[2048,128]{1,0:T(8,128)}, u32[]{:S(2)}) copy-start(f32[2048,128]{1,0:T(8,128)} %all-gather.7.cloned.1.call-done) | copy-start | bytes 3145732
  1236.1 2.0 copy-start
  1321.9 62.4 %copy-start.2 = (f32[32,512]{1,0:T(8,128)S(1)}, f32[32,512]{1,0:T(8,128)}, u32[]{:S(2)}) copy-start(f32[32,512]{1,0:T(8,128)} %param.136) | copy-start | bytes 196612
  1321.9 62.4 %copy-start.3 = (s32[32,512]{1,0:T(8,128)S(1)}, s32[32,512]{1,0:T(8,128)}, u32[]{:S(2)}) copy-start(s32[32,512]{1,0:T(8,128)} %param.137) | copy-start | bytes 196612
  1376.8 6.5 collective-permute-start.1
Sparse Core Ops, SparseCore 0:
  16.4 73.9 all-gather.8
  100.4 43.9 all-reduce.6
  151.1 141.5 reduce-scatter.2
  298.6 238.8 all-reduce.8
  563.8 74.1 all-gather.4
  643.9 43.9 all-reduce.10
  694.6 141.5 reduce-scatter.4
  842.3 238.8 all-reduce.12
  1107.5 74.1 all-gather.6
  1187.7 43.9 all-reduce.14
where the time goes:
time: 1400 us; the launch traced here: 1390 us
  waiting for transfers between devices  1040 us (74%)
  other arithmetic  234 us (17%)
  local copies, waits for them, and re-layouts  46 us (3%)
  matrix products  45.7 us (3%)
  between operations  15.6 us (1%)
    psum x2, waiting for transfers between devices, shards(): gram_matrix = lax.psum(local_gram, ('rows', 'coil'))  486 us
    reduce_scatter x2, waiting for transfers between devices, shards(): lax.psum_scatter(lax.dot_general(hankel_cols, images, (((1,), (1,)), ((),...  283 us
    another operation x128, other arithmetic  139 us
    all_gather x2, waiting for transfers between devices, apply_hankel(): lax.all_gather(current, 'rows', axis=0, tiled=True)  102 us
    psum x3, waiting for transfers between devices, coil_total(): return lax.psum(partial_value, 'coil')  89.5 us
    all_gather x1, waiting for transfers between devices, shards(): lax.all_gather(owned_basis, 'rows', axis=0, tiled=True)  74.2 us
    unnamed x63, other arithmetic  45.3 us
    scatter-add x64, local copies, waits for them, and re-layouts, shards(): spread = spread.at[:, offset:offset + tile_rows].add(stacked[offset])  43.2 us
  transfers between devices with their start and end apart: 12, of which 12 were waited for; matrix products, arithmetic and copies ran while one was open for 6% of the time, Pallas kernels for 0%

commit v1 on v0

--- a/solution.py
+++ b/solution.py
@@ -69,7 +69,7 @@
         local_gram = jnp.dot(
             normal_rows.T, normal_rows, precision=highest, preferred_element_type=jnp.float32
         )
-        gram_matrix = lax.psum(local_gram, ("rows", "coil"))
+        gram_matrix = lax.psum(lax.psum(local_gram, "coil"), "rows")
         owned_basis = orthonormal(normal_rows, gram_matrix)
     images = apply_hankel(owned_basis)
     projected = jnp.dot(

time: 1400 us -> 1360 us (0.971)
  waiting for transfers between devices: 1040 us -> 995 us
    psum x2 -> x4, waiting for transfers between devices: 486 us -> 440 us  [shards(): gram_matrix = lax.psum(lax.psum(local_gram, 'coil'), 'rows')]
  transfers between devices with their start and end apart: 12 -> 14, of which waited for: 12 -> 14; matrix products, arithmetic and copies ran while one was open for 6% -> 7% of each run, Pallas kernels for 0% -> 0%
where the time goes in v1:
time: 1360 us; the launch traced here: 1350 us
  waiting for transfers between devices  995 us (73%)
  other arithmetic  234 us (17%)
  local copies, waits for them, and re-layouts  46 us (3%)
  matrix products  45.7 us (3%)
  between operations  15.7 us (1%)
    psum x4, waiting for transfers between devices, shards(): gram_matrix = lax.psum(lax.psum(local_gram, 'coil'), 'rows')  440 us
    reduce_scatter x2, waiting for transfers between devices, shards(): lax.psum_scatter(lax.dot_general(hankel_cols, images, (((1,), (1,)), ((),...  283 us
    another operation x128, other arithmetic  139 us
    all_gather x2, waiting for transfers between devices, apply_hankel(): lax.all_gather(current, 'rows', axis=0, tiled=True)  102 us
    psum x3, waiting for transfers between devices, coil_total(): return lax.psum(partial_value, 'coil')  89.5 us
    all_gather x1, waiting for transfers between devices, shards(): lax.all_gather(owned_basis, 'rows', axis=0, tiled=True)  73.9 us
    unnamed x63, other arithmetic  45.3 us
    scatter-add x64, local copies, waits for them, and re-layouts, shards(): spread = spread.at[:, offset:offset + tile_rows].add(stacked[offset])  43.2 us
  transfers between devices with their start and end apart: 14, of which 14 were waited for; matrix products, arithmetic and copies ran while one was open for 7% of the time, Pallas kernels for 0%

profile of v1, /device:TPU:16, one launch (start us, length us, event | category | flops | bytes accessed | tf_op | source)
XLA Modules:
  0.0 1345.6 jit_solution(18267408769081180647)
XLA Ops:
  8.7 7.5 collective-permute-start
  62.2 28.1 %all-gather.9.cloned.1.call-done = f32[1,2048,128]{2,1,0:T(8,128)} async-done(((f32[1,32,128]{2,1,0:T(8,128)}), f32[1,2048,128]{2,1,0:T(8,128)}) %all-gather.9.cloned.1.call-update) | async-done | bytes 1048592 | tf_op jit(solution)/shard_map/all_gather | solution.py:52
  90.4 9.9 convolution_bitcast_fusion
  100.5 43.9 %all-reduce.9.cloned.1.call-done = f32[128,512]{0,1:T(8,128)} async-done(((f32[128,512]{0,1:T(8,128)}), f32[128,512]{0,1:T(8,128)}) %all-reduce.9.cloned.1.call-update) | async-done | bytes 262160 | tf_op jit(solution)/shard_map/psum | solution.py:25
  144.4 6.6 fusion.135
  151.0 141.7 %reduce-scatter.3.cloned.1.call-done = f32[32,128]{1,0:T(8,128)} async-done(((f32[2048,128]{1,0:T(8,128)}), f32[32,128]{1,0:T(8,128)}) %reduce-scatter.3.cloned.1.call-update) | async-done | bytes 16400 | tf_op jit(solution)/shard_map/reduce_scatter | solution.py:57
  294.5 44.7 %all-reduce.11.cloned.1.call-done = f32[128,128]{0,1:T(8,128)} async-done(((f32[128,128]{0,1:T(8,128)}), f32[128,128]{0,1:T(8,128)}) %all-reduce.11.cloned.1.call-update) | async-done | bytes 65552 | tf_op jit(solution)/shard_map/psum | solution.py:72
  339.2 175.4 %all-reduce.13.cloned.1.call-done = f32[128,128]{0,1:T(8,128)} async-done(((f32[128,128]{0,1:T(8,128)}), f32[128,128]{0,1:T(8,128)}) %all-reduce.13.cloned.1.call-update) | async-done | bytes 65552 | tf_op jit(solution)/shard_map/psum | solution.py:72
  516.4 11.7 cholesky.44
  529.4 9.8 custom-call.6
  541.0 73.7 %all-gather.5.cloned.1.call-done = f32[2048,128]{1,0:T(8,128)} async-done(((f32[32,128]{1,0:T(8,128)}), f32[2048,128]{1,0:T(8,128)}) %all-gather.5.cloned.1.call-update) | async-done | bytes 1048592 | tf_op jit(solution)/shard_map/all_gather | solution.py:52
  614.7 5.8 fusion.137
  620.6 44.0 %all-reduce.15.cloned.1.call-done = f32[128,512]{1,0:T(8,128)} async-done(((f32[128,512]{1,0:T(8,128)}), f32[128,512]{1,0:T(8,128)}) %all-reduce.15.cloned.1.call-update) | async-done | bytes 262160 | tf_op jit(solution)/shard_map/psum | solution.py:25
  664.6 6.6 fusion.138
  671.3 141.7 %reduce-scatter.5.cloned.1.call-done = f32[32,128]{1,0:T(8,128)} async-done(((f32[2048,128]{1,0:T(8,128)}), f32[32,128]{1,0:T(8,128)}) %reduce-scatter.5.cloned.1.call-update) | async-done | bytes 16400 | tf_op jit(solution)/shard_map/reduce_scatter | solution.py:57
  813.0 1.7 fusion.139
  814.8 44.8 %all-reduce.17.cloned.1.call-done = f32[128,128]{0,1:T(8,128)} async-done(((f32[128,128]{0,1:T(8,128)}), f32[128,128]{0,1:T(8,128)}) %all-reduce.17.cloned.1.call-update) | async-done | bytes 65552 | tf_op jit(solution)/shard_map/psum | solution.py:72
  860.1 174.9 %all-reduce.19.cloned.1.call-done = f32[128,128]{0,1:T(8,128)} async-done(((f32[128,128]{0,1:T(8,128)}), f32[128,128]{0,1:T(8,128)}) %all-reduce.19.cloned.1.call-update) | async-done | bytes 65552 | tf_op jit(solution)/shard_map/psum | solution.py:72
  1036.8 11.7 cholesky.55
  1049.9 9.8 custom-call.7
  1061.2 73.9 %all-gather.7.cloned.1.call-done = f32[2048,128]{1,0:T(8,128)} async-done(((f32[32,128]{1,0:T(8,128)}), f32[2048,128]{1,0:T(8,128)}) %all-gather.7.cloned.1.call-update) | async-done | bytes 1048592 | tf_op jit(solution)/shard_map/all_gather | solution.py:76
  1135.1 5.9 fusion.140
  1185.2 4.5 fusion.141
  1331.6 5.2 collective-permute-done.1
  (310 shorter events, 246.4 us)
Async XLA Ops:
  7.2 83.2 %all-gather.9.cloned.1.call-start = ((), (), s32[]{:S(2)}) async-start(), calls=%async_computation.13 | async-start | bytes 1064960 | tf_op jit(solution)/shard_map/all_gather | solution.py:52
  8.7 8.9 collective-permute-start
  16.2 128.1 %all-reduce.9.cloned.1.call-start = ((), (), s32[]{:S(2)}) async-start(), calls=%async_computation.2 | async-start | bytes 524288 | tf_op jit(solution)/shard_map/psum | solution.py:25
  100.3 192.4 %reduce-scatter.3.cloned.1.call-start = ((), (), s32[]{:S(2)}) async-start(), calls=%async_computation.3 | async-start | bytes 1064960 | tf_op jit(solution)/shard_map/reduce_scatter | solution.py:57
  151.0 188.2 %all-reduce.11.cloned.1.call-start = ((), (), s32[]{:S(2)}) async-start(), calls=%async_computation.4 | async-start | bytes 131072 | tf_op jit(solution)/shard_map/psum | solution.py:72
  294.4 220.1 %all-reduce.13.cloned.1.call-start = ((), (), s32[]{:S(2)}) async-start(), calls=%async_computation.5 | async-start | bytes 131072 | tf_op jit(solution)/shard_map/psum | solution.py:72
  339.2 275.5 %all-gather.5.cloned.1.call-start = ((), (), s32[]{:S(2)}) async-start(), calls=%async_computation.6 | async-start | bytes 1064960 | tf_op jit(solution)/shard_map/all_gather | solution.py:52
  540.8 123.8 %all-reduce.15.cloned.1.call-start = ((), (), s32[]{:S(2)}) async-start(), calls=%async_computation.7 | async-start | bytes 524288 | tf_op jit(solution)/shard_map/psum | solution.py:25
  620.5 192.5 %reduce-scatter.5.cloned.1.call-start = ((), (), s32[]{:S(2)}) async-start(), calls=%async_computation.8 | async-start | bytes 1064960 | tf_op jit(solution)/shard_map/reduce_scatter | solution.py:57
  671.3 188.3 %all-reduce.17.cloned.1.call-start = ((), (), s32[]{:S(2)}) async-start(), calls=%async_computation.9 | async-start | bytes 131072 | tf_op jit(solution)/shard_map/psum | solution.py:72
  814.7 220.3 %all-reduce.19.cloned.1.call-start = ((), (), s32[]{:S(2)}) async-start(), calls=%async_computation.10 | async-start | bytes 131072 | tf_op jit(solution)/shard_map/psum | solution.py:72
  859.6 275.5 %all-gather.7.cloned.1.call-start = ((), (), s32[]{:S(2)}) async-start(), calls=%async_computation.11 | async-start | bytes 1064960 | tf_op jit(solution)/shard_map/all_gather | solution.py:76
  1061.2 124.0 %all-reduce.21.cloned.1.call-start = ((), (), s32[]{:S(2)}) async-start(), calls=%async_computation.12 | async-start | bytes 524288 | tf_op jit(solution)/shard_map/psum | solution.py:25
  1135.1 50.0 %copy-start.1 = (f32[2048,128]{1,0:T(8,128)S(1)}, f32[2048,128]{1,0:T(8,128)}, u32[]{:S(2)}) copy-start(f32[2048,128]{1,0:T(8,128)} %all-gather.7.cloned.1.call-done) | copy-start | bytes 3145732
  1189.6 2.0 copy-start
  1275.4 62.4 %copy-start.2 = (f32[32,512]{1,0:T(8,128)S(1)}, f32[32,512]{1,0:T(8,128)}, u32[]{:S(2)}) copy-start(f32[32,512]{1,0:T(8,128)} %param.136) | copy-start | bytes 196612
  1275.4 62.4 %copy-start.3 = (s32[32,512]{1,0:T(8,128)S(1)}, s32[32,512]{1,0:T(8,128)}, u32[]{:S(2)}) copy-start(s32[32,512]{1,0:T(8,128)} %param.137) | copy-start | bytes 196612
  1330.3 6.5 collective-permute-start.1
Sparse Core Ops, SparseCore 0:
  16.4 73.9 all-gather.8
  100.4 43.9 all-reduce.8
  151.1 141.5 reduce-scatter.2
  295.4 43.6 all-reduce.10
  342.5 172.0 all-reduce.12
  540.9 73.7 all-gather.4
  620.6 43.9 all-reduce.14
  671.4 141.5 reduce-scatter.4
  815.9 43.6 all-reduce.16
  862.9 172.0 all-reduce.18
  1061.3 73.7 all-gather.6
  1141.2 43.9 all-reduce.20
